TPU v7x, 32 devices: a whole 2x2x4 slice. The times are simulated.
32 devices in a mesh: ray: 4 (over x, core), vox: 8 (over z, y).
Axes of the slice: x: 2, y: 2, z: 4, core: 2. Of those that a mesh axis runs over, the one named last changes fastest.
Arguments:
- tiles: float32 [2048, 128, 128], P(('ray', 'vox')), may hold values from -0.25 to 0.25
- tile_ray: int32 [2048], P(('ray', 'vox')), may hold values from 0 to 15
- tile_vox: int32 [2048], P(('ray', 'vox')), may hold values from 0 to 511, as said below
- tile_count: int32 [32], P(('ray', 'vox')), may hold values from 1 to 64, as said below
- travel: float32 [512, 128], P(('ray', 'vox')), may hold values from -6 to 6
Outputs:
- solution: float32 [512, 128], P('vox')
- direction: float32 [512, 128], P('vox')
Inputs may be any that keep to these rules, and one draw needn't show every extreme that they name: `tile_count`: each entry is 1 to 64; some device has exactly 64 live slots. Among the 64 slots of one device (live or not), at most 16 have voxel blocks in the same range of 64 blocks (same tile_vox // 64); on every device some range is named by exactly 16 slots.
All inputs are finite; a program needn't handle non-finite values.
Results may differ from a plain program's by a relative error of at most 0.00017.
Values sent between devices are 32-bit elements; how exact they have to be, the bound alone decides.
No kernel may reach another device: no remote copies, remote signals or barrier semaphores. Data moves between devices by JAX's collectives and lax.ppermute only.
A program may use at most 64 MiB of HBM per device.

v0:
```python
import jax
import jax.numpy as jnp
from jax import lax
from jax.sharding import PartitionSpec as P

VBD = 64
ITERS = 2
HIGH = lax.Precision.HIGHEST


def on_device(tiles, tile_ray, tile_vox, tile_count, travel):
    n_vox = lax.axis_size("vox")
    blocks_all = VBD * n_vox
    tile_num = tiles.shape[0]
    ray_blocks = travel.shape[0]
    width = travel.shape[1]
    live = (jnp.arange(tile_num, dtype=jnp.int32) < tile_count[0]).astype(jnp.float32)[:, None]
    selector = (tile_ray[None, :] == jnp.arange(ray_blocks, dtype=jnp.int32)[:, None]).astype(
        jnp.float32
    )

    def backward(ray_vec):
        rows_in = jnp.dot(selector.T, ray_vec, precision=HIGH)
        prod = jnp.einsum("tij,ti->tj", tiles, rows_in, precision=HIGH) * live
        partial_sum = jnp.zeros((blocks_all, width), jnp.float32).at[tile_vox].add(prod)
        owned = lax.psum_scatter(partial_sum, "vox", scatter_dimension=0, tiled=True)
        return lax.psum(owned, "ray")

    def ray_length(ray_vec):
        return jnp.sqrt(lax.psum(jnp.sum(ray_vec * ray_vec), ("ray", "vox")))

    def vox_length(vox_vec):
        return jnp.sqrt(lax.psum(jnp.sum(vox_vec * vox_vec), "vox"))

    beta_now = ray_length(travel)
    ray_vec = travel / beta_now
    vox_vec = backward(ray_vec)
    alpha_now = vox_length(vox_vec)
    vox_vec = vox_vec / alpha_now
    direction = vox_vec
    solution = jnp.zeros_like(vox_vec)
    phibar = beta_now
    rhobar = alpha_now
    for step in range(ITERS):
        whole = lax.all_gather(vox_vec, "vox", axis=0, tiled=True)
        forward_prod = jnp.einsum("tij,tj->ti", tiles, whole[tile_vox], precision=HIGH) * live
        ray_vec = jnp.dot(selector, forward_prod, precision=HIGH) - alpha_now * ray_vec
        beta_now = ray_length(ray_vec)
        ray_vec = ray_vec / beta_now
        vox_vec = backward(ray_vec) - beta_now * vox_vec
        alpha_now = vox_length(vox_vec)
        vox_vec = vox_vec / alpha_now
        rho_val = jnp.sqrt(rhobar * rhobar + beta_now * beta_now)
        cosine = rhobar / rho_val
        sine_val = beta_now / rho_val
        theta_val = sine_val * alpha_now
        rhobar = -cosine * alpha_now
        phi_val = cosine * phibar
        phibar = sine_val * phibar
        solution = solution + phi_val / rho_val * direction
        direction = vox_vec - theta_val / rho_val * direction
    return (solution, direction)


def solution(mesh):
    return jax.shard_map(
        on_device,
        mesh=mesh,
        in_specs=(
            P(("ray", "vox"), None, None),
            P(("ray", "vox")),
            P(("ray", "vox")),
            P(("ray", "vox")),
            P(("ray", "vox"), None),
        ),
        out_specs=(P("vox", None), P("vox", None)),
        check_vma=False,
    )
```

profile of v0, /device:TPU:0, one launch (start us, length us, event | category | flops | bytes accessed | tf_op | source)
XLA Modules:
  0.0 524.3 jit_solution(6376675607895804721)
XLA Ops:
  7.2 1.3 multiply_reduce_fusion.5
  8.5 42.2 %psum.63 = f32[]{:T(128)} all-reduce(f32[]{:T(128)} %multiply_reduce_fusion.5), channel_id=1, replica_groups=mesh['ray'=4,'vox'=8] {'ray','vox'}, use_global_device_ids=true, to_apply=%region_1.0 | all-reduce | flops 1 | bytes 8 | tf_op jit(solution)/shard_map/psum | solution.py:30
  51.4 0.7 compare_select_fusion
  52.7 0.9 fusion.19
  53.7 5.3 %fusion.26 = f32[64,1,128]{2,1,0:T(1,128)S(1)} fusion(f32[64,128,1]{1,2,0:T(1,128)S(1)} %bitcast.43, f32[64,128,128]{2,1,0:T(8,128)} %param.5), kind=kOutput, calls=%fused_computation.52 | convolution fusion | flops 12582912 | bytes 4259840 | tf_op jit(solution)/shard_map/tij,ti->tj/dot_general | solution.py:24
  59.0 1.5 scatter_custom_fusion
  60.6 61.7 %reduce-scatter.4.cloned.1.call-done = f32[64,128]{1,0:T(8,128)} async-done(((f32[512,128]{1,0:T(8,128)}), f32[64,128]{1,0:T(8,128)}) %reduce-scatter.4.cloned.1.call-update) | async-done | bytes 32784 | tf_op jit(solution)/shard_map/reduce_scatter | solution.py:26
  122.3 10.8 %psum.64 = f32[64,128]{1,0:T(8,128)S(1)} all-reduce(f32[64,128]{1,0:T(8,128)} %reduce-scatter.4.cloned.1.call-done), channel_id=1, replica_groups=mesh['ray'=4,'vox'=8] {'ray'}, use_global_device_ids=true, to_apply=%region_4.0 | all-reduce | flops 8192 | bytes 65536 | tf_op jit(solution)/shard_map/psum | solution.py:27
  133.1 0.6 multiply_reduce_fusion.2
  133.7 20.1 %psum.65 = f32[]{:T(128)} all-reduce(f32[]{:T(128)} %multiply_reduce_fusion.2), channel_id=1, replica_groups=mesh['ray'=4,'vox'=8] {'vox'}, use_global_device_ids=true, to_apply=%region_6.0 | all-reduce | flops 1 | bytes 8 | tf_op jit(solution)/shard_map/psum | solution.py:33
  154.5 30.9 %all_gather.6 = f32[512,128]{1,0:T(8,128)S(1)} all-gather(f32[64,128]{1,0:T(8,128)S(1)} %broadcast_divide_fusion.1), channel_id=1, replica_groups=mesh['ray'=4,'vox'=8] {'vox'}, dimensions={0}, use_global_device_ids=true | all-gather | bytes 294912 | tf_op jit(solution)/shard_map/all_gather | solution.py:45
  185.4 0.6 gather_fusion
  186.0 8.3 %fusion.27 = f32[64,1,128]{2,1,0:T(1,128)S(1)} fusion(f32[64,128,1]{1,2,0:T(1,128)S(1)} %bitcast.40, f32[64,128,128]{2,1,0:T(8,128)} %param.5), kind=kOutput, calls=%fused_computation.53 | convolution fusion | flops 12582912 | bytes 4259840 | tf_op jit(solution)/shard_map/tij,tj->ti/dot_general | solution.py:46
  194.3 0.8 multiply_reduce_fusion.4
  195.2 37.1 %psum.66 = f32[]{:T(128)} all-reduce(f32[]{:T(128)} %get-tuple-element.4), channel_id=1, replica_groups=mesh['ray'=4,'vox'=8] {'ray','vox'}, use_global_device_ids=true, to_apply=%region_8.0 | all-reduce | flops 1 | bytes 8 | tf_op jit(solution)/shard_map/psum | solution.py:30
  233.2 5.3 %fusion.28 = f32[64,1,128]{2,1,0:T(1,128)S(1)} fusion(f32[64,128,1]{1,2,0:T(1,128)S(1)} %bitcast.44, f32[64,128,128]{2,1,0:T(8,128)} %param.5), kind=kOutput, calls=%fused_computation.54 | convolution fusion | flops 12582912 | bytes 4259840 | tf_op jit(solution)/shard_map/tij,ti->tj/dot_general | solution.py:24
  238.5 1.5 scatter_custom_fusion.1
  240.1 63.4 %reduce-scatter.6.cloned.1.call-done = f32[64,128]{1,0:T(8,128)} async-done(((f32[512,128]{1,0:T(8,128)}), f32[64,128]{1,0:T(8,128)}) %reduce-scatter.6.cloned.1.call-update) | async-done | bytes 32784 | tf_op jit(solution)/shard_map/reduce_scatter | solution.py:26
  303.4 10.8 %psum.67 = f32[64,128]{1,0:T(8,128)S(1)} all-reduce(f32[64,128]{1,0:T(8,128)} %reduce-scatter.6.cloned.1.call-done), channel_id=1, replica_groups=mesh['ray'=4,'vox'=8] {'ray'}, use_global_device_ids=true, to_apply=%region_11.0 | all-reduce | flops 8192 | bytes 65536 | tf_op jit(solution)/shard_map/psum | solution.py:27
  314.2 0.6 multiply_reduce_fusion.1
  314.9 20.1 %psum.68 = f32[]{:T(128)} all-reduce(f32[]{:T(128)} %multiply_reduce_fusion.1), channel_id=1, replica_groups=mesh['ray'=4,'vox'=8] {'vox'}, use_global_device_ids=true, to_apply=%region_13.0 | all-reduce | flops 1 | bytes 8 | tf_op jit(solution)/shard_map/psum | solution.py:33
  335.7 31.1 %all_gather.7 = f32[512,128]{1,0:T(8,128)S(1)} all-gather(f32[64,128]{1,0:T(8,128)S(1)} %broadcast_divide_fusion), channel_id=1, replica_groups=mesh['ray'=4,'vox'=8] {'vox'}, dimensions={0}, use_global_device_ids=true | all-gather | bytes 294912 | tf_op jit(solution)/shard_map/all_gather | solution.py:45
  367.3 8.3 %fusion.29 = f32[64,1,128]{2,1,0:T(1,128)S(1)} fusion(f32[64,128,1]{1,2,0:T(1,128)S(1)} %bitcast.38, f32[64,128,128]{2,1,0:T(8,128)} %param.5), kind=kOutput, calls=%fused_computation.55 | convolution fusion | flops 12582912 | bytes 4259840 | tf_op jit(solution)/shard_map/tij,tj->ti/dot_general | solution.py:46
  375.6 0.8 multiply_reduce_fusion.3
  376.4 37.1 %psum.69 = f32[]{:T(128)} all-reduce(f32[]{:T(128)} %get-tuple-element.6), channel_id=1, replica_groups=mesh['ray'=4,'vox'=8] {'ray','vox'}, use_global_device_ids=true, to_apply=%region_15.0 | all-reduce | flops 1 | bytes 8 | tf_op jit(solution)/shard_map/psum | solution.py:30
  414.5 5.3 %fusion.30 = f32[64,1,128]{2,1,0:T(1,128)S(1)} fusion(f32[64,128,1]{1,2,0:T(1,128)S(1)} %bitcast.42, f32[64,128,128]{2,1,0:T(8,128)} %param.5), kind=kOutput, calls=%fused_computation.56 | convolution fusion | flops 12582912 | bytes 4259840 | tf_op jit(solution)/shard_map/tij,ti->tj/dot_general | solution.py:24
  419.8 1.5 scatter_custom_fusion.2
  421.7 63.1 %reduce-scatter.8.cloned.1.call-done = f32[64,128]{1,0:T(8,128)} async-done(((f32[512,128]{1,0:T(8,128)}), f32[64,128]{1,0:T(8,128)}) %reduce-scatter.8.cloned.1.call-update) | async-done | bytes 32784 | tf_op jit(solution)/shard_map/reduce_scatter | solution.py:26
  484.8 10.8 %psum.70 = f32[64,128]{1,0:T(8,128)S(1)} all-reduce(f32[64,128]{1,0:T(8,128)} %reduce-scatter.8.cloned.1.call-done), channel_id=1, replica_groups=mesh['ray'=4,'vox'=8] {'ray'}, use_global_device_ids=true, to_apply=%region_18.0 | all-reduce | flops 8192 | bytes 65536 | tf_op jit(solution)/shard_map/psum | solution.py:27
  495.6 0.6 multiply_reduce_fusion
  496.2 20.1 %psum.71 = f32[]{:T(128)} all-reduce(f32[]{:T(128)} %multiply_reduce_fusion), channel_id=1, replica_groups=mesh['ray'=4,'vox'=8] {'vox'}, use_global_device_ids=true, to_apply=%region_20.0 | all-reduce | flops 1 | bytes 8 | tf_op jit(solution)/shard_map/psum | solution.py:33
  517.1 0.7 multiply_subtract_fusion
  (17 shorter events, 1.2 us)
Async XLA Ops:
  7.2 115.2 %reduce-scatter.4.cloned.1.call-start = ((), (), s32[]{:S(2)}) async-start(), calls=%async_computation.3 | async-start | bytes 294912 | tf_op jit(solution)/shard_map/reduce_scatter | solution.py:26
  53.7 140.7 %copy-start = (f32[16,128]{1,0:T(8,128)S(1)}, f32[16,128]{1,0:T(8,128)}, u32[]{:S(2)}) copy-start(f32[16,128]{1,0:T(8,128)} %param.9) | copy-start | bytes 24580
  53.7 140.7 %copy-start.1 = (s32[64]{0:T(128)S(1)}, s32[64]{0:T(128)}, u32[]{:S(2)}) copy-start(s32[64]{0:T(128)} %param.6) | copy-start | bytes 772
  60.5 242.9 %reduce-scatter.6.cloned.1.call-start = ((), (), s32[]{:S(2)}) async-start(), calls=%async_computation.4 | async-start | bytes 294912 | tf_op jit(solution)/shard_map/reduce_scatter | solution.py:26
  240.0 244.7 %reduce-scatter.8.cloned.1.call-start = ((), (), s32[]{:S(2)}) async-start(), calls=%async_computation.5 | async-start | bytes 294912 | tf_op jit(solution)/shard_map/reduce_scatter | solution.py:26
Sparse Core Ops, SparseCore 0:
  60.7 61.6 reduce-scatter.3
  240.2 63.2 reduce-scatter.5
  421.5 63.2 reduce-scatter.7
where the time goes:
time: 526 us; the launch traced here: 524 us
  blocking collectives  271 us (52%)
  waiting for transfers between devices  188 us (36%)
  matrix products  35.5 us (7%)
  between operations  19.1 us (4%)
  other arithmetic  9.11 us (2%)
    reduce_scatter x3, waiting for transfers between devices, backward(): lax.psum_scatter(partial_sum, 'vox', scatter_dimension=0, tiled=True)  188 us
    psum x3, blocking collectives, ray_length(): return jnp.sqrt(lax.psum(jnp.sum(ray_vec * ray_vec), ('ray', 'vox')))  116 us
    all_gather x2, blocking collectives, on_device(): whole = lax.all_gather(vox_vec, 'vox', axis=0, tiled=True)  62 us
    psum x3, blocking collectives, vox_length(): return jnp.sqrt(lax.psum(jnp.sum(vox_vec * vox_vec), 'vox'))  60.2 us
    psum x3, blocking collectives, backward(): return lax.psum(owned, 'ray')  32.4 us
    dot_general x2, matrix products, on_device(): jnp.einsum('tij,tj->ti', tiles, whole[tile_vox], precision=HIGH) * live  16.6 us
    dot_general x3, matrix products, backward(): prod = jnp.einsum('tij,ti->tj', tiles, rows_in, precision=HIGH) * live  15.8 us
  transfers between devices with their start and end apart: 3, of which 3 were waited for; matrix products, arithmetic and copies ran while one was open for 0% of the time, Pallas kernels for 0%

commit v1 on v0

--- a/solution.py
+++ b/solution.py
@@ -42,7 +42,14 @@
     phibar = beta_now
     rhobar = alpha_now
     for step in range(ITERS):
-        whole = lax.all_gather(vox_vec, "vox", axis=0, tiled=True)
+        ring = [vox_vec]
+        for hop in range(7):
+            ring.append(lax.ppermute(ring[-1], "vox", [(dev, (dev + 1) % 8) for dev in range(8)]))
+        whole = jnp.roll(
+            jnp.concatenate(ring[::-1], axis=0),
+            (lax.axis_index("vox") + 1) * ring[0].shape[0],
+            axis=0,
+        )
         forward_prod = jnp.einsum("tij,tj->ti", tiles, whole[tile_vox], precision=HIGH) * live
         ray_vec = jnp.dot(selector, forward_prod, precision=HIGH) - alpha_now * ray_vec
         beta_now = ray_length(ray_vec)

time: 526 us -> 557 us (1.059)
  waiting for transfers between devices: 188 us -> 281 us
  blocking collectives: 271 us -> 209 us
    ppermute x0 -> x14, waiting for transfers between devices: none -> 92.6 us  [on_device(): lax.ppermute(ring[-1], 'vox', [(dev, (dev + 1) % 8) for dev in range(8)])]
    all_gather x2 -> x0, blocking collectives: 62 us -> none  [on_device(): whole = lax.all_gather(vox_vec, 'vox', axis=0, tiled=True)]
  transfers between devices with their start and end apart: 3 -> 17, of which waited for: 3 -> 17; matrix products, arithmetic and copies ran while one was open for 0% -> 0% of each run, Pallas kernels for 0% -> 0%
where the time goes in v1:
time: 557 us; the launch traced here: 556 us
  waiting for transfers between devices  281 us (50%)
  blocking collectives  209 us (38%)
  matrix products  35.5 us (6%)
  between operations  19.2 us (3%)
  other arithmetic  9.45 us (2%)
    reduce_scatter x3, waiting for transfers between devices, backward(): lax.psum_scatter(partial_sum, 'vox', scatter_dimension=0, tiled=True)  189 us
    psum x3, blocking collectives, ray_length(): return jnp.sqrt(lax.psum(jnp.sum(ray_vec * ray_vec), ('ray', 'vox')))  116 us
    ppermute x14, waiting for transfers between devices, on_device(): lax.ppermute(ring[-1], 'vox', [(dev, (dev + 1) % 8) for dev in range(8)])  92.6 us
    psum x3, blocking collectives, vox_length(): return jnp.sqrt(lax.psum(jnp.sum(vox_vec * vox_vec), 'vox'))  60.2 us
    psum x3, blocking collectives, backward(): return lax.psum(owned, 'ray')  32.4 us
    dot_general x2, matrix products, on_device(): jnp.einsum('tij,tj->ti', tiles, whole[tile_vox], precision=HIGH) * live  16.6 us
    dot_general x3, matrix products, backward(): prod = jnp.einsum('tij,ti->tj', tiles, rows_in, precision=HIGH) * live  15.8 us
  transfers between devices with their start and end apart: 17, of which 17 were waited for; matrix products, arithmetic and copies ran while one was open for 0% of the time, Pallas kernels for 0%

profile of v1, /device:TPU:0, one launch (start us, length us, event | category | flops | bytes accessed | tf_op | source)
XLA Modules:
  0.0 555.9 jit_solution(8006494841622293227)
XLA Ops:
  8.5 42.2 %psum.63 = f32[]{:T(128)} all-reduce(f32[]{:T(128)} %multiply_reduce_fusion.5), channel_id=1, replica_groups=mesh['ray'=4,'vox'=8] {'ray','vox'}, use_global_device_ids=true, to_apply=%region_1.0 | all-reduce | flops 1 | bytes 8 | tf_op jit(solution)/shard_map/psum | solution.py:30
  53.7 5.3 fusion.28
  58.9 1.5 scatter_custom_fusion
  60.6 61.7 %reduce-scatter.4.cloned.1.call-done = f32[64,128]{1,0:T(8,128)} async-done(((f32[512,128]{1,0:T(8,128)}), f32[64,128]{1,0:T(8,128)}) %reduce-scatter.4.cloned.1.call-update) | async-done | bytes 32784 | tf_op jit(solution)/shard_map/reduce_scatter | solution.py:26
  122.3 10.8 %psum.64 = f32[64,128]{1,0:T(8,128)S(1)} all-reduce(f32[64,128]{1,0:T(8,128)} %reduce-scatter.4.cloned.1.call-done), channel_id=1, replica_groups=mesh['ray'=4,'vox'=8] {'ray'}, use_global_device_ids=true, to_apply=%region_4.0 | all-reduce | flops 8192 | bytes 65536 | tf_op jit(solution)/shard_map/psum | solution.py:27
  133.7 20.1 %psum.65 = f32[]{:T(128)} all-reduce(f32[]{:T(128)} %multiply_reduce_fusion.2), channel_id=1, replica_groups=mesh['ray'=4,'vox'=8] {'vox'}, use_global_device_ids=true, to_apply=%region_6.0 | all-reduce | flops 1 | bytes 8 | tf_op jit(solution)/shard_map/psum | solution.py:33
  154.5 6.6 %collective-permute-done = f32[64,128]{1,0:T(8,128)S(1)} collective-permute-done((f32[64,128]{1,0:T(8,128)S(1)}, f32[64,128]{1,0:T(8,128)S(1)}, u32[]{:S(2)}, u32[]{:S(2)}) %collective-permute-start) | collective-permute-done | bytes 32800 | tf_op jit(solution)/shard_map/ppermute | solution.py:47
  161.1 6.7 %collective-permute-done.1 = f32[64,128]{1,0:T(8,128)S(1)} collective-permute-done((f32[64,128]{1,0:T(8,128)S(1)}, f32[64,128]{1,0:T(8,128)S(1)}, u32[]{:S(2)}, u32[]{:S(2)}) %collective-permute-start.1) | collective-permute-done | bytes 32800 | tf_op jit(solution)/shard_map/ppermute | solution.py:47
  167.8 6.6 %collective-permute-done.2 = f32[64,128]{1,0:T(8,128)S(1)} collective-permute-done((f32[64,128]{1,0:T(8,128)S(1)}, f32[64,128]{1,0:T(8,128)S(1)}, u32[]{:S(2)}, u32[]{:S(2)}) %collective-permute-start.2) | collective-permute-done | bytes 32800 | tf_op jit(solution)/shard_map/ppermute | solution.py:47
  174.4 6.6 %collective-permute-done.3 = f32[64,128]{1,0:T(8,128)S(1)} collective-permute-done((f32[64,128]{1,0:T(8,128)S(1)}, f32[64,128]{1,0:T(8,128)S(1)}, u32[]{:S(2)}, u32[]{:S(2)}) %collective-permute-start.3) | collective-permute-done | bytes 32800 | tf_op jit(solution)/shard_map/ppermute | solution.py:47
  181.1 6.6 %collective-permute-done.4 = f32[64,128]{1,0:T(8,128)S(1)} collective-permute-done((f32[64,128]{1,0:T(8,128)S(1)}, f32[64,128]{1,0:T(8,128)S(1)}, u32[]{:S(2)}, u32[]{:S(2)}) %collective-permute-start.4) | collective-permute-done | bytes 32800 | tf_op jit(solution)/shard_map/ppermute | solution.py:47
  187.7 6.6 %collective-permute-done.5 = f32[64,128]{1,0:T(8,128)S(1)} collective-permute-done((f32[64,128]{1,0:T(8,128)S(1)}, f32[64,128]{1,0:T(8,128)S(1)}, u32[]{:S(2)}, u32[]{:S(2)}) %collective-permute-start.5) | collective-permute-done | bytes 32800 | tf_op jit(solution)/shard_map/ppermute | solution.py:47
  194.3 6.6 %collective-permute-done.6 = f32[64,128]{1,0:T(8,128)S(1)} collective-permute-done((f32[64,128]{1,0:T(8,128)S(1)}, f32[64,128]{1,0:T(8,128)S(1)}, u32[]{:S(2)}, u32[]{:S(2)}) %collective-permute-start.6) | collective-permute-done | bytes 32800 | tf_op jit(solution)/shard_map/ppermute | solution.py:47
  201.8 8.3 %fusion.29 = f32[64,1,128]{2,1,0:T(1,128)S(1)} fusion(f32[64,128,1]{1,2,0:T(1,128)S(1)} %bitcast.40, f32[64,128,128]{2,1,0:T(8,128)} %param.7), kind=kOutput, calls=%fused_computation.75 | convolution fusion | flops 12582912 | bytes 4259840 | tf_op jit(solution)/shard_map/tij,tj->ti/dot_general | solution.py:53
  210.9 37.1 %psum.66 = f32[]{:T(128)} all-reduce(f32[]{:T(128)} %get-tuple-element.5), channel_id=1, replica_groups=mesh['ray'=4,'vox'=8] {'ray','vox'}, use_global_device_ids=true, to_apply=%region_8.10 | all-reduce | flops 1 | bytes 8 | tf_op jit(solution)/shard_map/psum | solution.py:30
  248.9 5.3 fusion.30
  255.8 63.6 %reduce-scatter.6.cloned.1.call-done = f32[64,128]{1,0:T(8,128)} async-done(((f32[512,128]{1,0:T(8,128)}), f32[64,128]{1,0:T(8,128)}) %reduce-scatter.6.cloned.1.call-update) | async-done | bytes 32784 | tf_op jit(solution)/shard_map/reduce_scatter | solution.py:26
  319.4 10.8 %psum.67 = f32[64,128]{1,0:T(8,128)S(1)} all-reduce(f32[64,128]{1,0:T(8,128)} %reduce-scatter.6.cloned.1.call-done), channel_id=1, replica_groups=mesh['ray'=4,'vox'=8] {'ray'}, use_global_device_ids=true, to_apply=%region_11.13 | all-reduce | flops 8192 | bytes 65536 | tf_op jit(solution)/shard_map/psum | solution.py:27
  330.8 20.0 %psum.68 = f32[]{:T(128)} all-reduce(f32[]{:T(128)} %multiply_reduce_fusion.1), channel_id=1, replica_groups=mesh['ray'=4,'vox'=8] {'vox'}, use_global_device_ids=true, to_apply=%region_13.15 | all-reduce | flops 1 | bytes 8 | tf_op jit(solution)/shard_map/psum | solution.py:33
  351.6 6.6 %collective-permute-done.7 = f32[64,128]{1,0:T(8,128)S(1)} collective-permute-done((f32[64,128]{1,0:T(8,128)S(1)}, f32[64,128]{1,0:T(8,128)S(1)}, u32[]{:S(2)}, u32[]{:S(2)}) %collective-permute-start.7) | collective-permute-done | bytes 32800 | tf_op jit(solution)/shard_map/ppermute | solution.py:47
  358.2 6.7 %collective-permute-done.8 = f32[64,128]{1,0:T(8,128)S(1)} collective-permute-done((f32[64,128]{1,0:T(8,128)S(1)}, f32[64,128]{1,0:T(8,128)S(1)}, u32[]{:S(2)}, u32[]{:S(2)}) %collective-permute-start.8) | collective-permute-done | bytes 32800 | tf_op jit(solution)/shard_map/ppermute | solution.py:47
  364.9 6.6 %collective-permute-done.9 = f32[64,128]{1,0:T(8,128)S(1)} collective-permute-done((f32[64,128]{1,0:T(8,128)S(1)}, f32[64,128]{1,0:T(8,128)S(1)}, u32[]{:S(2)}, u32[]{:S(2)}) %collective-permute-start.9) | collective-permute-done | bytes 32800 | tf_op jit(solution)/shard_map/ppermute | solution.py:47
  371.5 6.6 %collective-permute-done.10 = f32[64,128]{1,0:T(8,128)S(1)} collective-permute-done((f32[64,128]{1,0:T(8,128)S(1)}, f32[64,128]{1,0:T(8,128)S(1)}, u32[]{:S(2)}, u32[]{:S(2)}) %collective-permute-start.10) | collective-permute-done | bytes 32800 | tf_op jit(solution)/shard_map/ppermute | solution.py:47
  378.1 6.6 %collective-permute-done.11 = f32[64,128]{1,0:T(8,128)S(1)} collective-permute-done((f32[64,128]{1,0:T(8,128)S(1)}, f32[64,128]{1,0:T(8,128)S(1)}, u32[]{:S(2)}, u32[]{:S(2)}) %collective-permute-start.11) | collective-permute-done | bytes 32800 | tf_op jit(solution)/shard_map/ppermute | solution.py:47
  384.7 6.6 %collective-permute-done.12 = f32[64,128]{1,0:T(8,128)S(1)} collective-permute-done((f32[64,128]{1,0:T(8,128)S(1)}, f32[64,128]{1,0:T(8,128)S(1)}, u32[]{:S(2)}, u32[]{:S(2)}) %collective-permute-start.12) | collective-permute-done | bytes 32800 | tf_op jit(solution)/shard_map/ppermute | solution.py:47
  391.3 6.6 %collective-permute-done.13 = f32[64,128]{1,0:T(8,128)S(1)} collective-permute-done((f32[64,128]{1,0:T(8,128)S(1)}, f32[64,128]{1,0:T(8,128)S(1)}, u32[]{:S(2)}, u32[]{:S(2)}) %collective-permute-start.13) | collective-permute-done | bytes 32800 | tf_op jit(solution)/shard_map/ppermute | solution.py:47
  398.8 8.3 %fusion.31 = f32[64,1,128]{2,1,0:T(1,128)S(1)} fusion(f32[64,128,1]{1,2,0:T(1,128)S(1)} %bitcast.38, f32[64,128,128]{2,1,0:T(8,128)} %param.7), kind=kOutput, calls=%fused_computation.77 | convolution fusion | flops 12582912 | bytes 4259840 | tf_op jit(solution)/shard_map/tij,tj->ti/dot_general | solution.py:53
  407.9 37.1 %psum.69 = f32[]{:T(128)} all-reduce(f32[]{:T(128)} %get-tuple-element.7), channel_id=1, replica_groups=mesh['ray'=4,'vox'=8] {'ray','vox'}, use_global_device_ids=true, to_apply=%region_15.17 | all-reduce | flops 1 | bytes 8 | tf_op jit(solution)/shard_map/psum | solution.py:30
  445.9 5.3 fusion.32
  453.1 63.2 %reduce-scatter.8.cloned.1.call-done = f32[64,128]{1,0:T(8,128)} async-done(((f32[512,128]{1,0:T(8,128)}), f32[64,128]{1,0:T(8,128)}) %reduce-scatter.8.cloned.1.call-update) | async-done | bytes 32784 | tf_op jit(solution)/shard_map/reduce_scatter | solution.py:26
  516.4 10.8 %psum.70 = f32[64,128]{1,0:T(8,128)S(1)} all-reduce(f32[64,128]{1,0:T(8,128)} %reduce-scatter.8.cloned.1.call-done), channel_id=1, replica_groups=mesh['ray'=4,'vox'=8] {'ray'}, use_global_device_ids=true, to_apply=%region_18.20 | all-reduce | flops 8192 | bytes 65536 | tf_op jit(solution)/shard_map/psum | solution.py:27
  527.8 20.1 %psum.71 = f32[]{:T(128)} all-reduce(f32[]{:T(128)} %multiply_reduce_fusion), channel_id=1, replica_groups=mesh['ray'=4,'vox'=8] {'vox'}, use_global_device_ids=true, to_apply=%region_20.22 | all-reduce | flops 1 | bytes 8 | tf_op jit(solution)/shard_map/psum | solution.py:33
  (61 shorter events, 12.5 us)
Async XLA Ops:
  7.2 115.1 %reduce-scatter.4.cloned.1.call-start = ((), (), s32[]{:S(2)}) async-start(), calls=%async_computation.3 | async-start | bytes 294912 | tf_op jit(solution)/shard_map/reduce_scatter | solution.py:26
  58.9 151.1 %copy-start = (f32[16,128]{1,0:T(8,128)S(1)}, f32[16,128]{1,0:T(8,128)}, u32[]{:S(2)}) copy-start(f32[16,128]{1,0:T(8,128)} %param.11) | copy-start | bytes 24580
  58.9 151.1 %copy-start.1 = (s32[64]{0:T(128)S(1)}, s32[64]{0:T(128)}, u32[]{:S(2)}) copy-start(s32[64]{0:T(128)} %param.8) | copy-start | bytes 772
  60.5 258.8 %reduce-scatter.6.cloned.1.call-start = ((), (), s32[]{:S(2)}) async-start(), calls=%async_computation.4 | async-start | bytes 294912 | tf_op jit(solution)/shard_map/reduce_scatter | solution.py:26
  154.5 6.7 %collective-permute-start = (f32[64,128]{1,0:T(8,128)S(1)}, f32[64,128]{1,0:T(8,128)S(1)}, u32[]{:S(2)}, u32[]{:S(2)}) collective-permute-start(f32[64,128]{1,0:T(8,128)S(1)} %broadcast_divide_fusion.1), channel_id=1, source_target_pairs={{0,1},{1,2},{2,3},{3,4},{4,5},{5,6},{6,7},{7,0},{8,9},{9,10},{10,1... | collective-permute-start | bytes 98312 | tf_op jit(solution)/shard_map/ppermute | solution.py:47
  161.1 6.7 %collective-permute-start.1 = (f32[64,128]{1,0:T(8,128)S(1)}, f32[64,128]{1,0:T(8,128)S(1)}, u32[]{:S(2)}, u32[]{:S(2)}) collective-permute-start(f32[64,128]{1,0:T(8,128)S(1)} %collective-permute-done), channel_id=1, source_target_pairs={{0,1},{1,2},{2,3},{3,4},{4,5},{5,6},{6,7},{7,0},{8,9},{9,10},{10,1... | collective-permute-start | bytes 98312 | tf_op jit(solution)/shard_map/ppermute | solution.py:47
  167.8 6.6 %collective-permute-start.2 = (f32[64,128]{1,0:T(8,128)S(1)}, f32[64,128]{1,0:T(8,128)S(1)}, u32[]{:S(2)}, u32[]{:S(2)}) collective-permute-start(f32[64,128]{1,0:T(8,128)S(1)} %collective-permute-done.1), channel_id=1, source_target_pairs={{0,1},{1,2},{2,3},{3,4},{4,5},{5,6},{6,7},{7,0},{8,9},{9,10},{10,1... | collective-permute-start | bytes 98312 | tf_op jit(solution)/shard_map/ppermute | solution.py:47
  174.4 6.6 %collective-permute-start.3 = (f32[64,128]{1,0:T(8,128)S(1)}, f32[64,128]{1,0:T(8,128)S(1)}, u32[]{:S(2)}, u32[]{:S(2)}) collective-permute-start(f32[64,128]{1,0:T(8,128)S(1)} %collective-permute-done.2), channel_id=1, source_target_pairs={{0,1},{1,2},{2,3},{3,4},{4,5},{5,6},{6,7},{7,0},{8,9},{9,10},{10,1... | collective-permute-start | bytes 98312 | tf_op jit(solution)/shard_map/ppermute | solution.py:47
  181.1 6.6 %collective-permute-start.4 = (f32[64,128]{1,0:T(8,128)S(1)}, f32[64,128]{1,0:T(8,128)S(1)}, u32[]{:S(2)}, u32[]{:S(2)}) collective-permute-start(f32[64,128]{1,0:T(8,128)S(1)} %collective-permute-done.3), channel_id=1, source_target_pairs={{0,1},{1,2},{2,3},{3,4},{4,5},{5,6},{6,7},{7,0},{8,9},{9,10},{10,1... | collective-permute-start | bytes 98312 | tf_op jit(solution)/shard_map/ppermute | solution.py:47
  187.7 6.6 %collective-permute-start.5 = (f32[64,128]{1,0:T(8,128)S(1)}, f32[64,128]{1,0:T(8,128)S(1)}, u32[]{:S(2)}, u32[]{:S(2)}) collective-permute-start(f32[64,128]{1,0:T(8,128)S(1)} %collective-permute-done.4), channel_id=1, source_target_pairs={{0,1},{1,2},{2,3},{3,4},{4,5},{5,6},{6,7},{7,0},{8,9},{9,10},{10,1... | collective-permute-start | bytes 98312 | tf_op jit(solution)/shard_map/ppermute | solution.py:47
  194.3 6.6 %collective-permute-start.6 = (f32[64,128]{1,0:T(8,128)S(1)}, f32[64,128]{1,0:T(8,128)S(1)}, u32[]{:S(2)}, u32[]{:S(2)}) collective-permute-start(f32[64,128]{1,0:T(8,128)S(1)} %collective-permute-done.5), channel_id=1, source_target_pairs={{0,1},{1,2},{2,3},{3,4},{4,5},{5,6},{6,7},{7,0},{8,9},{9,10},{10,1... | collective-permute-start | bytes 98312 | tf_op jit(solution)/shard_map/ppermute | solution.py:47
  255.8 260.6 %reduce-scatter.8.cloned.1.call-start = ((), (), s32[]{:S(2)}) async-start(), calls=%async_computation.5 | async-start | bytes 294912 | tf_op jit(solution)/shard_map/reduce_scatter | solution.py:26
  351.5 6.7 %collective-permute-start.7 = (f32[64,128]{1,0:T(8,128)S(1)}, f32[64,128]{1,0:T(8,128)S(1)}, u32[]{:S(2)}, u32[]{:S(2)}) collective-permute-start(f32[64,128]{1,0:T(8,128)S(1)} %broadcast_divide_fusion), channel_id=1, source_target_pairs={{0,1},{1,2},{2,3},{3,4},{4,5},{5,6},{6,7},{7,0},{8,9},{9,10},{10,1... | collective-permute-start | bytes 98312 | tf_op jit(solution)/shard_map/ppermute | solution.py:47
  358.2 6.7 %collective-permute-start.8 = (f32[64,128]{1,0:T(8,128)S(1)}, f32[64,128]{1,0:T(8,128)S(1)}, u32[]{:S(2)}, u32[]{:S(2)}) collective-permute-start(f32[64,128]{1,0:T(8,128)S(1)} %collective-permute-done.7), channel_id=1, source_target_pairs={{0,1},{1,2},{2,3},{3,4},{4,5},{5,6},{6,7},{7,0},{8,9},{9,10},{10,1... | collective-permute-start | bytes 98312 | tf_op jit(solution)/shard_map/ppermute | solution.py:47
  364.9 6.6 %collective-permute-start.9 = (f32[64,128]{1,0:T(8,128)S(1)}, f32[64,128]{1,0:T(8,128)S(1)}, u32[]{:S(2)}, u32[]{:S(2)}) collective-permute-start(f32[64,128]{1,0:T(8,128)S(1)} %collective-permute-done.8), channel_id=1, source_target_pairs={{0,1},{1,2},{2,3},{3,4},{4,5},{5,6},{6,7},{7,0},{8,9},{9,10},{10,1... | collective-permute-start | bytes 98312 | tf_op jit(solution)/shard_map/ppermute | solution.py:47
  371.5 6.6 %collective-permute-start.10 = (f32[64,128]{1,0:T(8,128)S(1)}, f32[64,128]{1,0:T(8,128)S(1)}, u32[]{:S(2)}, u32[]{:S(2)}) collective-permute-start(f32[64,128]{1,0:T(8,128)S(1)} %collective-permute-done.9), channel_id=1, source_target_pairs={{0,1},{1,2},{2,3},{3,4},{4,5},{5,6},{6,7},{7,0},{8,9},{9,10},{10,1... | collective-permute-start | bytes 98312 | tf_op jit(solution)/shard_map/ppermute | solution.py:47
  378.1 6.6 %collective-permute-start.11 = (f32[64,128]{1,0:T(8,128)S(1)}, f32[64,128]{1,0:T(8,128)S(1)}, u32[]{:S(2)}, u32[]{:S(2)}) collective-permute-start(f32[64,128]{1,0:T(8,128)S(1)} %collective-permute-done.10), channel_id=1, source_target_pairs={{0,1},{1,2},{2,3},{3,4},{4,5},{5,6},{6,7},{7,0},{8,9},{9,10},{10,1... | collective-permute-start | bytes 98312 | tf_op jit(solution)/shard_map/ppermute | solution.py:47
  384.7 6.6 %collective-permute-start.12 = (f32[64,128]{1,0:T(8,128)S(1)}, f32[64,128]{1,0:T(8,128)S(1)}, u32[]{:S(2)}, u32[]{:S(2)}) collective-permute-start(f32[64,128]{1,0:T(8,128)S(1)} %collective-permute-done.11), channel_id=1, source_target_pairs={{0,1},{1,2},{2,3},{3,4},{4,5},{5,6},{6,7},{7,0},{8,9},{9,10},{10,1... | collective-permute-start | bytes 98312 | tf_op jit(solution)/shard_map/ppermute | solution.py:47
  391.3 6.6 %collective-permute-start.13 = (f32[64,128]{1,0:T(8,128)S(1)}, f32[64,128]{1,0:T(8,128)S(1)}, u32[]{:S(2)}, u32[]{:S(2)}) collective-permute-start(f32[64,128]{1,0:T(8,128)S(1)} %collective-permute-done.12), channel_id=1, source_target_pairs={{0,1},{1,2},{2,3},{3,4},{4,5},{5,6},{6,7},{7,0},{8,9},{9,10},{10,1... | collective-permute-start | bytes 98312 | tf_op jit(solution)/shard_map/ppermute | solution.py:47
Sparse Core Ops, SparseCore 0:
  60.6 61.6 reduce-scatter.3
  255.9 63.4 reduce-scatter.5
  452.9 63.4 reduce-scatter.7
